TPU v7x, 32 devices: a whole 2x2x4 slice. The times are simulated.
32 devices in a mesh: ctx: 16 (over z, y, core), sec: 2 (over x).
Axes of the slice: x: 2, y: 2, z: 4, core: 2. Of those that a mesh axis runs over, the one named last changes fastest.
Arguments:
- query_nope: bfloat16 [1024, 8192], P('ctx', 'sec'), may hold values from -6 to 6
- query_rope: bfloat16 [1024, 4096], P('ctx', 'sec'), may hold values from -8 to 8
- key_latent: bfloat16 [1024, 512], P('ctx'), may hold values from -6 to 6
- key_rope: bfloat16 [1024, 64], P('ctx'), may hold values from -8 to 8
- key_up: bfloat16 [64, 512, 128], P('sec'), may hold values from -0.25 to 0.25
- value_up: bfloat16 [64, 512, 128], P('sec'), may hold values from -1 to 1
- routed_tokens: bfloat16 [4096, 7168], P(('ctx', 'sec')), may hold values from -6 to 6
- expert_ids: int32 [4096, 8], P(('ctx', 'sec')), may hold values from 0 to 255, as said below
- expert_gates: float32 [4096, 8], P(('ctx', 'sec')), may hold values from 0.2 to 2
- gate_weight: bfloat16 [7168, 8192], P(None, ('ctx', 'sec')), may hold values from -0.0625 to 0.0625
- up_weight: bfloat16 [7168, 8192], P(None, ('ctx', 'sec')), may hold values from -0.0625 to 0.0625
- down_weight: bfloat16 [8192, 7168], P(('ctx', 'sec')), may hold values from -0.125 to 0.125
Outputs:
- attention_out: bfloat16 [1024, 8192], P('ctx', 'sec')
- routed_out: bfloat16 [4096, 7168], P(('ctx', 'sec'))
Inputs may be any that keep to these rules, and one draw needn't show every extreme that they name: `expert_ids`: each row names 8 different experts, at most one of them below 4. Within each aligned block of 128 rows (the rows of one device) no expert below 4 is named more than 4 times, and in every draw one expert below 4 is named exactly 4 times in every block.
All inputs are finite; a program needn't handle non-finite values.
Results may differ from a plain program's by a relative error of at most 0.008.
Values may be sent and summed in bfloat16 or wider, within the bound.
A program may use at most 192 MiB of HBM per device.

v0:
```python
import functools

import jax
import jax.numpy as jnp
from jax import lax
from jax.experimental import pallas as pl
from jax.experimental.pallas import tpu as pltpu
from jax.sharding import PartitionSpec as P

CAP = 4
SPLIT = 8
CHUNKS = 4
LOG2E = 1.4426950408889634
MESH_ID = pl.DeviceIdType.MESH
F32 = jnp.float32
BF16 = jnp.bfloat16
NT = (((1,), (1,)), ((), ()))


def kernel(
    dims,
    ids_ref,
    gates_ref,
    klat_ref,
    krope_ref,
    tok_hbm,
    qn_hbm,
    qr_hbm,
    ku_hbm,
    vu_hbm,
    gw_hbm,
    uw_hbm,
    dw_hbm,
    att_ref,
    resb,
    wmix,
    tok,
    qn,
    qr,
    ku,
    vu,
    gw,
    uw,
    dw,
    qcat,
    keys,
    outg,
    zbuf,
    arr,
    acc,
    part,
    r1,
    s1,
    r2,
    s2,
    r3,
    rbuf,
    load_sem,
    kz_send,
    kx_send,
    ky_send,
    kc_send,
    krecv,
    zsend,
    zrecv,
    asend,
    arecv,
    rsend,
    rrecv,
    bsend,
    brecv,
):
    groups, n_sec, rows, heads, lat, ropew, nope, hb = dims
    slots = groups * CAP
    width = tok.shape[1]
    cw = width // CHUNKS
    tokens = tok.shape[0]
    sent = lat + 2 * ropew
    ctx = lax.axis_index("ctx")
    sec = lax.axis_index("sec")
    me = ctx * n_sec + sec
    g = me // SPLIT
    m = lax.rem(me, SPLIT)
    bx = lax.rem(m, 2)
    bc = lax.rem(m // 2, 2)
    by = m // 4
    mx = m + 1 - 2 * bx
    mc = m + 2 - 4 * bc
    my = m + 4 - 8 * by
    mxy = mx + my - m

    def dev(group, member):
        index = group * SPLIT + member
        return (index // n_sec, lax.rem(index, n_sec))

    pending = []

    def rcopy(src, dst, ss, rs, target):
        return pltpu.make_async_remote_copy(
            src_ref=src, dst_ref=dst, send_sem=ss, recv_sem=rs,
            device_id=target, device_id_type=MESH_ID,
        )

    def send(src, dst, ss, rs, target):
        cp = rcopy(src, dst, ss, rs, target)
        cp.start()
        pending.append(cp)
        return cp

    nx, nc, ny = dev(g, mx), dev(g, mc), dev(g, my)
    others = [lax.rem(g + step, groups) for step in range(1, groups)]
    every = [g] + others

    tok_loads = []
    for c in range(CHUNKS):
        cols = pl.ds(c * cw, cw)
        tok_loads.append(
            pltpu.make_async_copy(tok_hbm.at[:, cols], tok.at[:, cols], load_sem.at[8 + c])
        )
        tok_loads[c].start()

    barrier = pltpu.get_barrier_semaphore()
    for target in [nx, nc, ny] + [dev(o, m) for o in others]:
        pl.semaphore_signal(barrier, inc=1, device_id=target, device_id_type=MESH_ID)

    pairs = [
        (qn_hbm, qn), (qr_hbm, qr), (ku_hbm, ku),
        (gw_hbm, gw), (uw_hbm, uw), (dw_hbm, dw), (vu_hbm, vu),
    ]
    loads = [None]
    for i, (a, b) in enumerate(pairs):
        loads.append(pltpu.make_async_copy(a, b, load_sem.at[i]))

    own_keys = keys.at[ctx]
    own_keys[:, :lat] = klat_ref[...]
    own_keys[:, lat:sent] = jnp.concatenate([krope_ref[...], krope_ref[...]], axis=1)

    pl.semaphore_wait(barrier, 3 + len(others))
    part_rows = rows // 2

    def kpiece(shard, which):
        return keys.at[shard, pl.ds(pl.multiple_of(which * part_rows, part_rows), part_rows), pl.ds(0, sent)]

    def kwhole(shard):
        return keys.at[shard, :, pl.ds(0, sent)]

    def kshard(group, member):
        return (group * SPLIT + member) // n_sec

    def ksend(group, member, which, sem, target):
        shard = kshard(group, member)
        piece = kpiece(shard, which)
        send(piece, piece, sem, krecv.at[shard, which], target)

    def karrive(group, member, which):
        shard = kshard(group, member)
        piece = kpiece(shard, which)
        rcopy(piece, piece, kz_send.at[0], krecv.at[shard, which], nx).wait_recv()

    for i, o in enumerate(others):
        ksend(g, m, bx, kz_send.at[i], dev(o, m))
    for which in range(2):
        ksend(g, m, which, kz_send.at[groups - 1 + which], ny)

    lanes = wmix.shape[1]
    row = lax.broadcasted_iota(jnp.int32, (lanes, tokens), 0)
    slot = row & (slots - 1)
    expert = slot // CAP
    matches = jnp.zeros((lanes, tokens), F32)
    gate = jnp.zeros((lanes, tokens), F32)
    for k in range(ids_ref.shape[0]):
        hit = ids_ref[k : k + 1, :] == expert
        matches = jnp.where(hit, 1.0, matches)
        gate = gate + jnp.where(hit, gates_ref[k : k + 1, :], 0.0)
    earlier = (
        lax.broadcasted_iota(jnp.int32, (tokens, tokens), 0)
        < lax.broadcasted_iota(jnp.int32, (tokens, tokens), 1)
    )
    rank = jnp.dot(
        matches.astype(BF16), jnp.where(earlier, 1.0, 0.0).astype(BF16), preferred_element_type=F32
    )
    chosen = jnp.where(rank == (slot & (CAP - 1)).astype(F32), matches, 0.0)
    picker = chosen[:slots].astype(BF16)

    for c in range(CHUNKS):
        tok_loads[c].wait()
        picked = jnp.dot(picker, tok[:, c * cw : (c + 1) * cw], preferred_element_type=F32)
        for e in range(groups):
            outg[c, e] = picked[e * CAP : (e + 1) * CAP].astype(BF16)
        for i, o in enumerate(others):
            send(outg.at[c, o], zbuf.at[c, g], zsend.at[c, i], zrecv.at[c, g], dev(o, m))

    for load in loads[1:4]:
        load.start()
    weight = chosen * gate
    w1 = weight.astype(BF16).astype(F32)
    w2 = (weight - w1).astype(BF16).astype(F32)
    w3 = weight - w1 - w2
    wmix[...] = jnp.where(
        row < slots, w1, jnp.where(row < 2 * slots, w2, jnp.where(row < 3 * slots, w3, 0.0))
    ).T.astype(BF16)

    maskw = keys.shape[2] - sent

    @pl.loop(0, keys.shape[0])
    def _(shard):
        key_place = shard * rows + lax.broadcasted_iota(jnp.int32, (rows, maskw), 0)
        query = lax.broadcasted_iota(jnp.int32, (rows, maskw), 1)
        hidden_key = (key_place > ctx * rows + query) & (query < rows)
        keys[shard, :, sent:] = jnp.where(hidden_key, -1e30, 0.0).astype(BF16)

    loads[1].wait()
    loads[2].wait()
    loads[3].wait()
    for load in loads[4:]:
        load.start()
    unit = jnp.where(
        lax.broadcasted_iota(jnp.int32, (rows, maskw), 0)
        == lax.broadcasted_iota(jnp.int32, (rows, maskw), 1),
        1.0,
        0.0,
    ).astype(BF16)

    def query_latents(first, last):
        @pl.loop(first, last)
        def _(p):
            rope = qr[:, pl.ds(pl.multiple_of(p * 2 * ropew, 2 * ropew), 2 * ropew)]
            low = lax.broadcasted_iota(jnp.int32, rope.shape, 1) < ropew
            for k in range(2):
                h = p * 2 + k
                q = qn[:, pl.ds(pl.multiple_of(h * nope, nope), nope)]
                latent = lax.dot_general(q, ku[h], NT, preferred_element_type=F32)
                place = pl.ds(pl.multiple_of(h * rows, rows), rows)
                qcat[place, :lat] = latent.astype(BF16)
                keep = low if k == 0 else jnp.logical_not(low)
                qcat[place, lat:sent] = jnp.where(keep, rope.astype(F32), 0.0).astype(BF16)
                qcat[place, sent:] = unit

    half_pairs = heads // 4
    query_latents(0, half_pairs)

    for i, o in enumerate(others):
        karrive(o, m, bx)
        ksend(o, m, bx, kx_send.at[i, 0], nx)
        ksend(o, m, bx, ky_send.at[i], ny)

    def spread(kind, member, c, target):
        piece = arr.at[c, member]
        send(piece, piece, asend.at[kind, c], arecv.at[c, member], target)

    def arrive(member, c):
        piece = arr.at[c, member]
        rcopy(piece, piece, asend.at[0, c], arecv.at[c, member], nx).wait_recv()

    def start_chunk(c):
        for i, o in enumerate(others):
            rcopy(outg.at[c, o], zbuf.at[c, o], zsend.at[c, i], zrecv.at[c, o], dev(o, m)).wait_recv()
        zbuf[c, g] = outg[c, g]
        blocks = [zbuf[c, e].astype(F32) for e in range(groups)]
        arr[c, m] = jnp.concatenate(blocks, axis=0).astype(BF16)
        spread(0, m, c, nx)
        spread(1, m, c, ny)
        spread(2, m, c, nc)

    def forward_chunk(c):
        arrive(mx, c)
        if c % 2 == 0:
            spread(3, mx, c, ny)
        spread(4, mx, c, nc)
        arrive(my, c)
        if c % 2 == 1:
            spread(3, my, c, nx)
        spread(5, my, c, nc)

    count = SPLIT * slots

    def finish_chunk(c):
        arrive(mxy, c)
        spread(6, mxy, c, nc)

    def gate_up(c):
        for member in (mc, mx + mc - m, my + mc - m, mxy + mc - m):
            arrive(member, c)
        x = arr[c].reshape(count, cw)
        g_part = jnp.dot(x, gw[c * cw : (c + 1) * cw], preferred_element_type=F32)
        u_part = jnp.dot(x, uw[c * cw : (c + 1) * cw], preferred_element_type=F32)
        if c == 0:
            acc[0] = g_part
            acc[1] = u_part
        else:
            acc[0] += g_part
            acc[1] += u_part

    start_chunk(0)
    start_chunk(1)
    for i, o in enumerate(others):
        karrive(o, my, bx)
        ksend(o, my, bx, kx_send.at[i, 1], nx)
    forward_chunk(0)
    start_chunk(2)
    forward_chunk(1)
    start_chunk(3)
    finish_chunk(0)
    forward_chunk(2)
    finish_chunk(1)
    forward_chunk(3)

    shard = kshard(g, m)
    send(kwhole(shard), kwhole(shard), kc_send.at[0, 0], krecv.at[shard, 0], nc)
    for i, o in enumerate(others):
        karrive(o, m, 1 - bx)
        shard = kshard(o, m)
        send(kwhole(shard), kwhole(shard), kc_send.at[i + 1, 0], krecv.at[shard, 0], nc)
    for i, o in enumerate(every):
        karrive(o, my, 1 - bx)
        if i == 0:
            karrive(o, my, bx)
        shard = kshard(o, my)
        send(kwhole(shard), kwhole(shard), kc_send.at[i, 1], krecv.at[shard, 0], nc)

    loads[4].wait()
    loads[5].wait()
    gate_up(0)
    finish_chunk(2)
    gate_up(1)
    finish_chunk(3)
    query_latents(half_pairs, heads // 2)
    gate_up(2)
    gate_up(3)
    gate_act = acc[0]
    hidden = (gate_act / (1.0 + jnp.exp(-gate_act)) * acc[1]).astype(BF16)

    c1, c2, c3 = [], [], []
    loads[6].wait()

    def down(c):
        value = jnp.dot(hidden, dw[:, c * cw : (c + 1) * cw], preferred_element_type=F32)
        part[c] = value.astype(BF16).reshape(2, 2, 2, slots, cw)
        c1.append(send(part.at[c, :, 1 - bc], r1.at[c], rsend.at[0, c], rrecv.at[0, c], nc))

    def sum_cores(c):
        c1[c].wait_recv()
        for a in range(2):
            for b in range(2):
                s1[c, a, b] = (part[c, a, bc, b].astype(F32) + r1[c, a, b].astype(F32)).astype(BF16)
        src = s1.at[c, :, 1 - bx] if c % 2 == 0 else s1.at[c, 1 - by]
        c2.append(send(src, r2.at[c], rsend.at[1, c], rrecv.at[1, c], nx if c % 2 == 0 else ny))

    def sum_first(c):
        c2[c].wait_recv()
        for a in range(2):
            mine = s1[c, a, bx] if c % 2 == 0 else s1[c, by, a]
            s2[c, a] = (mine.astype(F32) + r2[c, a].astype(F32)).astype(BF16)
        keep = by if c % 2 == 0 else bx
        c3.append(send(s2.at[c, 1 - keep], r3.at[c], rsend.at[2, c], rrecv.at[2, c],
                       ny if c % 2 == 0 else nx))

    def sum_second(c):
        c3[c].wait_recv()
        keep = by if c % 2 == 0 else bx
        total = s2[c, keep].astype(F32) + r3[c].astype(F32)
        for e in range(groups):
            rbuf[c, e] = total[e * CAP : (e + 1) * CAP].astype(BF16)
        for i, o in enumerate(others):
            send(rbuf.at[c, o], resb.at[c, g], bsend.at[c, i], brecv.at[c, g], dev(o, m))
        resb[c, g] = rbuf[c, g]

    for c in range(CHUNKS):
        down(c)

    loads[7].wait()
    for o in every:
        for member in (mc, my + mc - m):
            shard = kshard(o, member)
            rcopy(kwhole(shard), kwhole(shard), kc_send.at[0, 0], krecv.at[shard, 0], nc).wait_recv()

    seq = keys.shape[0] * keys.shape[1]
    block = hb * rows
    scale = (nope + ropew) ** -0.5 * LOG2E

    def attend(first, last):
        @pl.loop(first, last)
        def _(b):
            q = qcat[pl.ds(pl.multiple_of(b * block, block), block)]
            kk = keys[...].reshape(seq, keys.shape[2])
            score = lax.dot_general(q, kk, NT, preferred_element_type=F32)
            top = jnp.max(score, axis=1, keepdims=True)
            expo = jnp.exp2((score - top) * scale)
            total = jnp.sum(expo, axis=1, keepdims=True)
            mixed = jnp.dot(expo.astype(BF16), kk[:, :lat], preferred_element_type=F32)
            mixed = (mixed / total).astype(BF16)
            for k in range(hb):
                h = b * hb + k
                value = jnp.dot(
                    mixed[k * rows : (k + 1) * rows], vu[h], preferred_element_type=F32
                )
                vdim = value.shape[1]
                att_ref[:, pl.ds(pl.multiple_of(h * vdim, vdim), vdim)] = value.astype(BF16)

    nb = heads // hb
    eighth = nb // 8
    attend(0, eighth)
    for c in range(CHUNKS):
        sum_cores(c)
    attend(eighth, 3 * eighth)
    for c in range(CHUNKS):
        sum_first(c)
    attend(3 * eighth, 5 * eighth)
    for c in range(CHUNKS):
        sum_second(c)
    attend(5 * eighth, nb)

    for c in range(CHUNKS):
        for i, o in enumerate(others):
            rcopy(rbuf.at[c, o], resb.at[c, o], bsend.at[c, i], brecv.at[c, o], dev(o, m)).wait_recv()
    for cp in pending:
        cp.wait_send()


def finish(res_ref, wmix_ref, att_in, rout_ref, att_out):
    chunks, groups, _, cw = res_ref.shape
    att_out[...] = att_in[...]
    for c in range(chunks):
        blocks = [res_ref[c, e].astype(F32) for e in range(groups)]
        block_rows = jnp.concatenate(blocks, axis=0).astype(BF16)
        tall = jnp.concatenate([block_rows] * 3, axis=0)
        rout_ref[:, c * cw : (c + 1) * cw] = jnp.dot(
            wmix_ref[:, : tall.shape[0]], tall, preferred_element_type=F32
        ).astype(BF16)


def local(n_ctx, n_sec, qn, qr, klat, krope, ku, vu, tok, ids, gates, gw, uw, dw):
    devices = n_ctx * n_sec
    groups = devices // SPLIT
    slots = groups * CAP
    rows = qn.shape[0]
    heads, lat, nope = ku.shape
    ropew = krope.shape[1]
    tokens, width = tok.shape
    cw = width // CHUNKS
    kw = lat + 2 * ropew + 128
    hb = 4 if n_ctx * rows <= 2048 else 1
    lanes = -(-3 * slots // 128) * 128
    dims = (groups, n_sec, rows, heads, lat, ropew, nope, hb)
    v = pl.BlockSpec(memory_space=pltpu.VMEM)
    a = pl.BlockSpec(memory_space=pl.ANY)
    dma = pltpu.SemaphoreType.DMA
    out_width = heads * vu.shape[2]
    att, res, wmix = pl.pallas_call(
        functools.partial(kernel, dims),
        out_shape=(
            jax.ShapeDtypeStruct((rows, out_width), BF16),
            jax.ShapeDtypeStruct((CHUNKS, groups, CAP, cw), BF16),
            jax.ShapeDtypeStruct((tokens, lanes), BF16),
        ),
        in_specs=[v, v, v, v] + [a] * 8,
        out_specs=(v, v, v),
        scratch_shapes=[
            pltpu.VMEM(tok.shape, BF16),
            pltpu.VMEM(qn.shape, BF16),
            pltpu.VMEM(qr.shape, BF16),
            pltpu.VMEM(ku.shape, BF16),
            pltpu.VMEM(vu.shape, BF16),
            pltpu.VMEM(gw.shape, BF16),
            pltpu.VMEM(uw.shape, BF16),
            pltpu.VMEM(dw.shape, BF16),
            pltpu.VMEM((heads * rows, kw), BF16),
            pltpu.VMEM((n_ctx, rows, kw), BF16),
            pltpu.VMEM((CHUNKS, groups, CAP, cw), BF16),
            pltpu.VMEM((CHUNKS, groups, CAP, cw), BF16),
            pltpu.VMEM((CHUNKS, SPLIT, slots, cw), BF16),
            pltpu.VMEM((2, SPLIT * slots, gw.shape[1]), F32),
            pltpu.VMEM((CHUNKS, 2, 2, 2, slots, cw), BF16),
            pltpu.VMEM((CHUNKS, 2, 2, slots, cw), BF16),
            pltpu.VMEM((CHUNKS, 2, 2, slots, cw), BF16),
            pltpu.VMEM((CHUNKS, 2, slots, cw), BF16),
            pltpu.VMEM((CHUNKS, 2, slots, cw), BF16),
            pltpu.VMEM((CHUNKS, slots, cw), BF16),
            pltpu.VMEM((CHUNKS, groups, CAP, cw), BF16),
            dma((8 + CHUNKS,)),
            dma((groups + 1,)),
            dma((groups, 2)),
            dma((groups,)),
            dma((groups, 2)),
            dma((n_ctx, 2)),
            dma((CHUNKS, groups)),
            dma((CHUNKS, groups)),
            dma((7, CHUNKS)),
            dma((CHUNKS, SPLIT)),
            dma((3, CHUNKS)),
            dma((3, CHUNKS)),
            dma((CHUNKS, groups)),
            dma((CHUNKS, groups)),
        ],
        compiler_params=pltpu.CompilerParams(
            collective_id=0, has_side_effects=True, vmem_limit_bytes=67043328
        ),
    )(ids.T, gates.T, klat, krope, tok, qn, qr, ku, vu, gw, uw, dw)
    rout, att = pl.pallas_call(
        finish,
        out_shape=(jax.ShapeDtypeStruct(tok.shape, BF16), jax.ShapeDtypeStruct(att.shape, BF16)),
        in_specs=[v, v, v],
        out_specs=(v, v),
    )(res, wmix, att)
    return att, rout


def solution(mesh):
    body = functools.partial(local, mesh.shape["ctx"], mesh.shape["sec"])
    both = ("ctx", "sec")
    return jax.shard_map(
        body,
        mesh=mesh,
        in_specs=(
            P("ctx", "sec"),
            P("ctx", "sec"),
            P("ctx", None),
            P("ctx", None),
            P("sec", None, None),
            P("sec", None, None),
            P(both, None),
            P(both, None),
            P(both, None),
            P(None, both),
            P(None, both),
            P(both, None),
        ),
        out_specs=(P("ctx", "sec"), P(both, None)),
        check_vma=False,
    )
```

profile of v0, /device:TPU:0, one launch (start us, length us, event | category | flops | bytes accessed | tf_op | source)
XLA Modules:
  0.0 55.0 jit_solution(14177206781001371796)
XLA Ops:
  0.6 51.2 %shard_map.131 = (bf16[64,4096]{1,0:T(8,128)(2,1)}, bf16[4,4,4,1792]{3,2,1,0:T(4,128)(2,1)}, bf16[128,128]{1,0:T(8,128)(2,1)}) custom-call(s32[8,128]{1,0:T(8,128)} %bitcast.2, f32[8,128]{1,0:T(8,128)} %bitcast.3, bf16[64,512]{1,0:T(8,128)(2,1)} %klat_ref.1, bf16[64,64]{1,0:T(8,128)(2,1)} %krope_ref.1, bf16[128,7168]{1,0:T(8,128)(2,1)} %tok_hbm.1, ...), custom_call_target="tpu_custom_call" | custom-call | tf_op jit(solution)/shard_map/pallas_call | solution.py:449
  51.8 3.2 %shard_map.132 = (bf16[128,7168]{1,0:T(8,128)(2,1)}, bf16[64,4096]{1,0:T(8,128)(2,1)}) custom-call(bf16[4,4,4,1792]{3,2,1,0:T(4,128)(2,1)} %get-tuple-element.7.res_ref, bf16[128,128]{1,0:T(8,128)(2,1)} %get-tuple-element.8.wmix_ref, bf16[64,4096]{1,0:T(8,128)(2,1)} %get-tuple-element.9.att_in), custom_call_target="tpu_custom_call" | custom-call | tf_op jit(solution)/shard_map/pallas_call | solution.py:499
where the time goes:
time: 55.2 us; the launch traced here: 55 us
  Pallas kernels  54.3 us (98%)
  between operations  0.64 us (1%)
    pallas_call x1, Pallas kernels, local(): pl.pallas_call(functools.partial(kernel, dims), out_shape=(jax.ShapeDtype...  51.2 us
    pallas_call x1, Pallas kernels, local(): pl.pallas_call(finish, out_shape=(jax.ShapeDtypeStruct(tok.shape, BF16),...  3.16 us

commit v1 on v0

v1 whole, which is shorter than its diff:
```python
import functools

import jax
import jax.numpy as jnp
from jax import lax
from jax.experimental import pallas as pl
from jax.experimental.pallas import tpu as pltpu
from jax.sharding import PartitionSpec as P

CAP = 4
SPLIT = 8
CHUNKS = 4
RCHUNKS = 8
PIECES = 4
LOG2E = 1.4426950408889634
MESH_ID = pl.DeviceIdType.MESH
F32 = jnp.float32
BF16 = jnp.bfloat16
NT = (((1,), (1,)), ((), ()))
scope = jax.named_scope


def kernel(
    dims,
    ids_hbm,
    gates_hbm,
    klat_hbm,
    krope_hbm,
    tok_hbm,
    qn_hbm,
    qr_hbm,
    ku_hbm,
    vu_hbm,
    gw_hbm,
    uw_hbm,
    dw_hbm,
    att_hbm,
    res_hbm,
    wmix_hbm,
    ids_ref,
    gates_ref,
    krope_ref,
    wmix,
    att_ref,
    tok,
    qn,
    qr,
    ku,
    vu,
    gw,
    uw,
    dw,
    qcat,
    keys,
    outg,
    zbuf,
    arr,
    acc,
    part,
    r1,
    s1,
    r2,
    s2,
    r3,
    rbuf,
    load_sem,
    store_sem,
    kz_send,
    kx_send,
    ky_send,
    kc_send,
    krecv,
    zsend,
    zrecv,
    asend,
    arecv,
    rsend,
    rrecv,
    bsend,
    brecv,
):
    groups, n_sec, rows, heads, lat, ropew, nope, hb = dims
    slots = groups * CAP
    width = tok.shape[1]
    cw = width // CHUNKS
    rw = width // RCHUNKS
    tokens = tok.shape[0]
    sent = lat + 2 * ropew
    ctx = lax.axis_index("ctx")
    sec = lax.axis_index("sec")
    me = ctx * n_sec + sec
    g = me // SPLIT
    m = lax.rem(me, SPLIT)
    bx = lax.rem(m, 2)
    bc = lax.rem(m // 2, 2)
    by = m // 4
    mx = m + 1 - 2 * bx
    mc = m + 2 - 4 * bc
    my = m + 4 - 8 * by
    mxy = mx + my - m

    def dev(group, member):
        index = group * SPLIT + member
        return (index // n_sec, lax.rem(index, n_sec))

    pending = []
    stores = []

    def rcopy(src, dst, ss, rs, target):
        return pltpu.make_async_remote_copy(
            src_ref=src, dst_ref=dst, send_sem=ss, recv_sem=rs,
            device_id=target, device_id_type=MESH_ID,
        )

    def send(src, dst, ss, rs, target):
        cp = rcopy(src, dst, ss, rs, target)
        cp.start()
        pending.append(cp)
        return cp

    def store(src, dst):
        cp = pltpu.make_async_copy(src, dst, store_sem.at[len(stores)])
        cp.start()
        stores.append(cp)

    nx, nc, ny = dev(g, mx), dev(g, mc), dev(g, my)
    others = [lax.rem(g + step, groups) for step in range(1, groups)]
    every = [g] + others

    barrier = pltpu.get_barrier_semaphore()
    for target in [dev(o, m) for o in others] + [nx, nc, ny]:
        pl.semaphore_signal(barrier, inc=1, device_id=target, device_id_type=MESH_ID)

    own_keys = keys.at[ctx]
    pairs = [
        (ids_hbm, ids_ref), (gates_hbm, gates_ref), (qn_hbm, qn), (qr_hbm, qr), (ku_hbm, ku),
        (gw_hbm, gw), (uw_hbm, uw), (dw_hbm, dw), (vu_hbm, vu),
        (klat_hbm, own_keys.at[:, pl.ds(0, lat)]), (krope_hbm, krope_ref),
    ]
    loads = [pltpu.make_async_copy(a, b, load_sem.at[i]) for i, (a, b) in enumerate(pairs)]
    l_ids, l_gates, l_qn, l_qr, l_ku, l_gw, l_uw, l_dw, l_vu, l_klat, l_krope = loads
    l_ids.start()
    l_gates.start()
    tok_loads = []
    for c in range(CHUNKS):
        cols = pl.ds(c * cw, cw)
        tok_loads.append(
            pltpu.make_async_copy(
                tok_hbm.at[:, cols], tok.at[:, cols], load_sem.at[len(loads) + c]
            )
        )
        tok_loads[c].start()
    l_klat.start()
    l_krope.start()

    part_rows = rows // 2

    def kpiece(shard, which):
        return keys.at[shard, pl.ds(pl.multiple_of(which * part_rows, part_rows), part_rows), pl.ds(0, sent)]

    def kwhole(shard):
        return keys.at[shard, :, pl.ds(0, sent)]

    def kshard(group, member):
        return (group * SPLIT + member) // n_sec

    def ksend(group, member, which, sem, target):
        shard = kshard(group, member)
        piece = kpiece(shard, which)
        send(piece, piece, sem, krecv.at[shard, which], target)

    def karrive(group, member, which):
        shard = kshard(group, member)
        piece = kpiece(shard, which)
        rcopy(piece, piece, kz_send.at[0], krecv.at[shard, which], nx).wait_recv()

    def ksend_whole(group, member, sem, target):
        shard = kshard(group, member)
        send(kwhole(shard), kwhole(shard), sem, krecv.at[shard, 0], target)

    def karrive_whole(group, member):
        shard = kshard(group, member)
        rcopy(kwhole(shard), kwhole(shard), kz_send.at[0], krecv.at[shard, 0], nx).wait_recv()

    with scope("a_sel"):
        lanes = wmix.shape[1]
        row = lax.broadcasted_iota(jnp.int32, (lanes, tokens), 0)
        slot = row & (slots - 1)
        expert = slot // CAP
        matches = jnp.zeros((lanes, tokens), F32)
        gate = jnp.zeros((lanes, tokens), F32)
        l_ids.wait()
        l_gates.wait()
        for load in (l_qn, l_qr, l_ku):
            load.start()
        for k in range(ids_ref.shape[0]):
            hit = ids_ref[k : k + 1, :] == expert
            matches = jnp.where(hit, 1.0, matches)
            gate = gate + jnp.where(hit, gates_ref[k : k + 1, :], 0.0)
        earlier = (
            lax.broadcasted_iota(jnp.int32, (tokens, tokens), 0)
            < lax.broadcasted_iota(jnp.int32, (tokens, tokens), 1)
        )
        rank = jnp.dot(
            matches.astype(BF16), jnp.where(earlier, 1.0, 0.0).astype(BF16), preferred_element_type=F32
        )
        chosen = jnp.where(rank == (slot & (CAP - 1)).astype(F32), matches, 0.0)
        picker = chosen[:slots].astype(BF16)

    with scope("b_pick"):
        for c in range(CHUNKS):
            tok_loads[c].wait()
            picked = jnp.dot(picker, tok[:, c * cw : (c + 1) * cw], preferred_element_type=F32)
            for e in range(groups):
                outg[c, e] = picked[e * CAP : (e + 1) * CAP].astype(BF16)
        l_klat.wait()
        l_krope.wait()
        own_keys[:, lat:sent] = jnp.concatenate([krope_ref[...], krope_ref[...]], axis=1)

    with scope("c_barrier"):
        pl.semaphore_wait(barrier, 3 + len(others))

    with scope("d_zsend"):
        for c in range(CHUNKS):
            for i, o in enumerate(others):
                send(outg.at[c, o], zbuf.at[c, g], zsend.at[c, i], zrecv.at[c, g], dev(o, m))
        ksend(g, m, bx, ky_send.at[0], ny)
        for i, o in enumerate(others):
            ksend_whole(g, m, kz_send.at[i], dev(o, m))

    with scope("e_wmix"):
        weight = chosen * gate
        w1 = weight.astype(BF16).astype(F32)
        w2 = (weight - w1).astype(BF16).astype(F32)
        w3 = weight - w1 - w2
        wmix[...] = jnp.where(
            row < slots, w1, jnp.where(row < 2 * slots, w2, jnp.where(row < 3 * slots, w3, 0.0))
        ).T.astype(BF16)
        store(wmix, wmix_hbm)

        maskw = keys.shape[2] - sent

        @pl.loop(0, keys.shape[0])
        def _(shard):
            key_place = shard * rows + lax.broadcasted_iota(jnp.int32, (rows, maskw), 0)
            query = lax.broadcasted_iota(jnp.int32, (rows, maskw), 1)
            hidden_key = (key_place > ctx * rows + query) & (query < rows)
            keys[shard, :, sent:] = jnp.where(hidden_key, -1e30, 0.0).astype(BF16)

        unit = jnp.where(
            lax.broadcasted_iota(jnp.int32, (rows, maskw), 0)
            == lax.broadcasted_iota(jnp.int32, (rows, maskw), 1),
            1.0,
            0.0,
        ).astype(BF16)

    with scope("f_loads"):
        l_qn.wait()
        l_qr.wait()
        l_ku.wait()
        for load in (l_gw, l_uw, l_dw, l_vu):
            load.start()

    def query_latents(first, last):
        with scope("ql"):
            @pl.loop(first, last)
            def _(p):
                rope = qr[:, pl.ds(pl.multiple_of(p * 2 * ropew, 2 * ropew), 2 * ropew)]
                low = lax.broadcasted_iota(jnp.int32, rope.shape, 1) < ropew
                for k in range(2):
                    h = p * 2 + k
                    q = qn[:, pl.ds(pl.multiple_of(h * nope, nope), nope)]
                    latent = lax.dot_general(q, ku[h], NT, preferred_element_type=F32)
                    place = pl.ds(pl.multiple_of(h * rows, rows), rows)
                    qcat[place, :lat] = latent.astype(BF16)
                    keep = low if k == 0 else jnp.logical_not(low)
                    qcat[place, lat:sent] = jnp.where(keep, rope.astype(F32), 0.0).astype(BF16)
                    qcat[place, sent:] = unit

    def spread(kind, member, c, target):
        piece = arr.at[c, member]
        send(piece, piece, asend.at[kind, c], arecv.at[c, member], target)

    def arrive(member, c):
        piece = arr.at[c, member]
        rcopy(piece, piece, asend.at[0, c], arecv.at[c, member], nx).wait_recv()

    def start_chunk(c):
        with scope("s%d" % c):
            for i, o in enumerate(others):
                rcopy(outg.at[c, o], zbuf.at[c, o], zsend.at[c, i], zrecv.at[c, o], dev(o, m)).wait_recv()
            zbuf[c, g] = outg[c, g]
            blocks = [zbuf[c, e].astype(F32) for e in range(groups)]
            arr[c, m] = jnp.concatenate(blocks, axis=0).astype(BF16)
            spread(0, m, c, nx)
            spread(1, m, c, ny)
            spread(2, m, c, nc)

    def forward_chunk(c):
        with scope("fw%d" % c):
            arrive(mx, c)
            if c % 2 == 0:
                spread(3, mx, c, ny)
            spread(4, mx, c, nc)
            arrive(my, c)
            if c % 2 == 1:
                spread(3, my, c, nx)
            spread(5, my, c, nc)

    count = SPLIT * slots

    def finish_chunk(c):
        with scope("fin%d" % c):
            arrive(mxy, c)
            spread(6, mxy, c, nc)

    def gate_up(c):
        with scope("guw%d" % c):
            for member in (mc, mx + mc - m, my + mc - m, mxy + mc - m):
                arrive(member, c)
        with scope("gu%d" % c):
            x = arr[c].reshape(count, cw)
            g_part = jnp.dot(x, gw[c * cw : (c + 1) * cw], preferred_element_type=F32)
            u_part = jnp.dot(x, uw[c * cw : (c + 1) * cw], preferred_element_type=F32)
            if c == 0:
                acc[0] = g_part
                acc[1] = u_part
            else:
                acc[0] += g_part
                acc[1] += u_part

    def kx_own():
        with scope("kxo"):
            karrive(g, my, bx)
            ksend(g, my, bx, kx_send.at[0], nx)

    def ky_step():
        with scope("ky"):
            for i, o in enumerate(others):
                karrive_whole(o, m)
                ksend(o, m, bx, ky_send.at[i + 1], ny)

    def kx_step():
        with scope("kx"):
            for i, o in enumerate(others):
                karrive(o, my, bx)
                ksend(o, my, bx, kx_send.at[i + 1], nx)

    def kc_step():
        with scope("kc"):
            for i, o in enumerate(every):
                ksend_whole(o, m, kc_send.at[i, 0], nc)
            for i, o in enumerate(every):
                karrive(o, my, 1 - bx)
                ksend_whole(o, my, kc_send.at[i, 1], nc)

    def key_wait():
        with scope("kw"):
            for o in every:
                for member in (mc, my + mc - m):
                    karrive_whole(o, member)

    pairs_n = heads // 2

    def ql(a, b):
        query_latents(a * pairs_n // 8, b * pairs_n // 8)

    ql(0, 3)
    start_chunk(0)
    kx_own()
    ql(3, 4)
    start_chunk(1)
    ql(4, 5)
    forward_chunk(0)
    start_chunk(2)
    ql(5, 6)
    forward_chunk(1)
    start_chunk(3)
    finish_chunk(0)
    ql(6, 7)
    forward_chunk(2)
    l_gw.wait()
    l_uw.wait()
    finish_chunk(1)
    gate_up(0)
    forward_chunk(3)
    ky_step()
    finish_chunk(2)
    gate_up(1)
    ql(7, 8)
    finish_chunk(3)
    gate_up(2)
    kx_step()
    gate_up(3)
    with scope("act"):
        gate_act = acc[0]
        hidden = (gate_act / (1.0 + jnp.exp(-gate_act)) * acc[1]).astype(BF16)
        l_dw.wait()

    c1, c2, c3 = [], [], []

    def down(c):
        value = jnp.dot(hidden, dw[:, c * rw : (c + 1) * rw], preferred_element_type=F32)
        part[c] = value.astype(BF16).reshape(2, 2, 2, slots, rw)
        c1.append(send(part.at[c, :, 1 - bc], r1.at[c], rsend.at[0, c], rrecv.at[0, c], nc))

    def sum_cores(c):
        with scope("sc%d" % c):
            c1[c].wait_recv()
            for a in range(2):
                for b in range(2):
                    s1[c, a, b] = (part[c, a, bc, b].astype(F32) + r1[c, a, b].astype(F32)).astype(BF16)
            src = s1.at[c, :, 1 - bx] if c % 2 == 0 else s1.at[c, 1 - by]
            c2.append(send(src, r2.at[c], rsend.at[1, c], rrecv.at[1, c], nx if c % 2 == 0 else ny))

    def sum_first(c):
        with scope("sf%d" % c):
            c2[c].wait_recv()
            for a in range(2):
                mine = s1[c, a, bx] if c % 2 == 0 else s1[c, by, a]
                s2[c, a] = (mine.astype(F32) + r2[c, a].astype(F32)).astype(BF16)
            keep = by if c % 2 == 0 else bx
            c3.append(send(s2.at[c, 1 - keep], r3.at[c], rsend.at[2, c], rrecv.at[2, c],
                           ny if c % 2 == 0 else nx))

    def sum_second(c):
        with scope("ss%d" % c):
            c3[c].wait_recv()
            keep = by if c % 2 == 0 else bx
            total = s2[c, keep].astype(F32) + r3[c].astype(F32)
            for e in range(groups):
                rbuf[c, e] = total[e * CAP : (e + 1) * CAP].astype(BF16)
            for i, o in enumerate(others):
                send(rbuf.at[c, o], res_hbm.at[c, g], bsend.at[c, i], brecv.at[c, g], dev(o, m))
            store(rbuf.at[c, g], res_hbm.at[c, g])

    seq = keys.shape[0] * keys.shape[1]
    block = hb * rows
    scale = (nope + ropew) ** -0.5 * LOG2E
    nb = heads // hb
    vdim = vu.shape[2]

    def attend(a, b):
        first, last = a * nb // 8, b * nb // 8
        with scope("att%d" % a):
            @pl.loop(first, last)
            def _(b):
                q = qcat[pl.ds(pl.multiple_of(b * block, block), block)]
                kk = keys[...].reshape(seq, keys.shape[2])
                score = lax.dot_general(q, kk, NT, preferred_element_type=F32)
                top = jnp.max(score, axis=1, keepdims=True)
                expo = jnp.exp2((score - top) * scale)
                total = jnp.sum(expo, axis=1, keepdims=True)
                mixed = jnp.dot(expo.astype(BF16), kk[:, :lat], preferred_element_type=F32)
                mixed = (mixed / total).astype(BF16)
                for k in range(hb):
                    h = b * hb + k
                    value = jnp.dot(
                        mixed[k * rows : (k + 1) * rows], vu[h], preferred_element_type=F32
                    )
                    att_ref[:, pl.ds(pl.multiple_of(h * vdim, vdim), vdim)] = value.astype(BF16)

            cols = pl.ds(first * hb * vdim, (last - first) * hb * vdim)
            store(att_ref.at[:, cols], att_hbm.at[:, cols])

    def pair(fn, k):
        fn(2 * k)
        fn(2 * k + 1)

    with scope("down"):
        for c in range(RCHUNKS):
            down(c)
    pair(sum_cores, 0)
    pair(sum_cores, 1)
    kc_step()
    pair(sum_first, 0)
    pair(sum_cores, 2)
    with scope("vuw"):
        l_vu.wait()
    key_wait()
    attend(0, 1)
    pair(sum_first, 1)
    pair(sum_cores, 3)
    pair(sum_second, 0)
    attend(1, 2)
    pair(sum_first, 2)
    pair(sum_second, 1)
    attend(2, 3)
    pair(sum_first, 3)
    pair(sum_second, 2)
    attend(3, 5)
    pair(sum_second, 3)
    attend(5, 8)

    with scope("z_res"):
        for c in range(RCHUNKS):
            for i, o in enumerate(others):
                rcopy(rbuf.at[c, o], res_hbm.at[c, o], bsend.at[c, i], brecv.at[c, o], dev(o, m)).wait_recv()
    with scope("z_sends"):
        for cp in pending:
            cp.wait_send()
        for cp in stores:
            cp.wait()


def finish(res_hbm, wmix_hbm, att_hbm, rout_hbm, out_hbm, res, wmix, att, rout, sem):
    chunks, groups, _, cw = res.shape
    step = chunks // PIECES
    w_load = pltpu.make_async_copy(wmix_hbm, wmix, sem.at[0])
    w_load.start()
    loads = []
    for p in range(PIECES):
        piece = pl.ds(p * step, step)
        loads.append(pltpu.make_async_copy(res_hbm.at[piece], res.at[piece], sem.at[1 + p]))
        loads[p].start()
    a_load = pltpu.make_async_copy(att_hbm, att, sem.at[1 + PIECES])
    a_load.start()
    w_load.wait()
    stores = []
    for p in range(PIECES):
        loads[p].wait()
        for c in range(p * step, (p + 1) * step):
            blocks = [res[c, e].astype(F32) for e in range(groups)]
            block_rows = jnp.concatenate(blocks, axis=0).astype(BF16)
            tall = jnp.concatenate([block_rows] * 3, axis=0)
            rout[:, c * cw : (c + 1) * cw] = jnp.dot(
                wmix[:, : tall.shape[0]], tall, preferred_element_type=F32
            ).astype(BF16)
        cols = pl.ds(p * step * cw, step * cw)
        stores.append(
            pltpu.make_async_copy(rout.at[:, cols], rout_hbm.at[:, cols], sem.at[2 + PIECES + p])
        )
        stores[p].start()
    a_load.wait()
    stores.append(pltpu.make_async_copy(att, out_hbm, sem.at[2 + 2 * PIECES]))
    stores[-1].start()
    for cp in stores:
        cp.wait()


def local(n_ctx, n_sec, qn, qr, klat, krope, ku, vu, tok, ids, gates, gw, uw, dw):
    devices = n_ctx * n_sec
    groups = devices // SPLIT
    slots = groups * CAP
    rows = qn.shape[0]
    heads, lat, nope = ku.shape
    ropew = krope.shape[1]
    tokens, width = tok.shape
    cw = width // CHUNKS
    rw = width // RCHUNKS
    kw = lat + 2 * ropew + 128
    hb = 4 if n_ctx * rows <= 2048 else 1
    lanes = -(-3 * slots // 128) * 128
    dims = (groups, n_sec, rows, heads, lat, ropew, nope, hb)
    a = pl.BlockSpec(memory_space=pl.ANY)
    dma = pltpu.SemaphoreType.DMA
    out_width = heads * vu.shape[2]
    att, res, wmix = pl.pallas_call(
        functools.partial(kernel, dims),
        out_shape=(
            jax.ShapeDtypeStruct((rows, out_width), BF16),
            jax.ShapeDtypeStruct((RCHUNKS, groups, CAP, rw), BF16),
            jax.ShapeDtypeStruct((tokens, lanes), BF16),
        ),
        in_specs=[a] * 12,
        out_specs=(a, a, a),
        scratch_shapes=[
            pltpu.VMEM(ids.shape[::-1], ids.dtype),
            pltpu.VMEM(gates.shape[::-1], gates.dtype),
            pltpu.VMEM(krope.shape, BF16),
            pltpu.VMEM((tokens, lanes), BF16),
            pltpu.VMEM((rows, out_width), BF16),
            pltpu.VMEM(tok.shape, BF16),
            pltpu.VMEM(qn.shape, BF16),
            pltpu.VMEM(qr.shape, BF16),
            pltpu.VMEM(ku.shape, BF16),
            pltpu.VMEM(vu.shape, BF16),
            pltpu.VMEM(gw.shape, BF16),
            pltpu.VMEM(uw.shape, BF16),
            pltpu.VMEM(dw.shape, BF16),
            pltpu.VMEM((heads * rows, kw), BF16),
            pltpu.VMEM((n_ctx, rows, kw), BF16),
            pltpu.VMEM((CHUNKS, groups, CAP, cw), BF16),
            pltpu.VMEM((CHUNKS, groups, CAP, cw), BF16),
            pltpu.VMEM((CHUNKS, SPLIT, slots, cw), BF16),
            pltpu.VMEM((2, SPLIT * slots, gw.shape[1]), F32),
            pltpu.VMEM((RCHUNKS, 2, 2, 2, slots, rw), BF16),
            pltpu.VMEM((RCHUNKS, 2, 2, slots, rw), BF16),
            pltpu.VMEM((RCHUNKS, 2, 2, slots, rw), BF16),
            pltpu.VMEM((RCHUNKS, 2, slots, rw), BF16),
            pltpu.VMEM((RCHUNKS, 2, slots, rw), BF16),
            pltpu.VMEM((RCHUNKS, slots, rw), BF16),
            pltpu.VMEM((RCHUNKS, groups, CAP, rw), BF16),
            dma((11 + CHUNKS,)),
            dma((1 + RCHUNKS + 8,)),
            dma((groups,)),
            dma((groups,)),
            dma((groups,)),
            dma((groups, 2)),
            dma((n_ctx, 2)),
            dma((CHUNKS, groups)),
            dma((CHUNKS, groups)),
            dma((7, CHUNKS)),
            dma((CHUNKS, SPLIT)),
            dma((3, RCHUNKS)),
            dma((3, RCHUNKS)),
            dma((RCHUNKS, groups)),
            dma((RCHUNKS, groups)),
        ],
        compiler_params=pltpu.CompilerParams(
            collective_id=0, has_side_effects=True, vmem_limit_bytes=67043328
        ),
    )(ids.T, gates.T, klat, krope, tok, qn, qr, ku, vu, gw, uw, dw)
    rout, att = pl.pallas_call(
        finish,
        out_shape=(jax.ShapeDtypeStruct(tok.shape, BF16), jax.ShapeDtypeStruct(att.shape, BF16)),
        in_specs=[a, a, a],
        out_specs=(a, a),
        scratch_shapes=[
            pltpu.VMEM(res.shape, BF16),
            pltpu.VMEM(wmix.shape, BF16),
            pltpu.VMEM(att.shape, BF16),
            pltpu.VMEM(tok.shape, BF16),
            dma((3 + 2 * PIECES,)),
        ],
    )(res, wmix, att)
    return att, rout


def solution(mesh):
    body = functools.partial(local, mesh.shape["ctx"], mesh.shape["sec"])
    both = ("ctx", "sec")
    return jax.shard_map(
        body,
        mesh=mesh,
        in_specs=(
            P("ctx", "sec"),
            P("ctx", "sec"),
            P("ctx", None),
            P("ctx", None),
            P("sec", None, None),
            P("sec", None, None),
            P(both, None),
            P(both, None),
            P(both, None),
            P(None, both),
            P(None, both),
            P(both, None),
        ),
        out_specs=(P("ctx", "sec"), P(both, None)),
        check_vma=False,
    )
```

time: 55.2 us -> 50.4 us (0.913)
  Pallas kernels: 54.3 us -> 49.6 us
    pallas_call x1, Pallas kernels: 51.2 us -> 46.7 us  [local(): pl.pallas_call(functools.partial(kernel, dims), out_shape=(jax.ShapeDtype...]
where the time goes in v1:
time: 50.4 us; the launch traced here: 50.2 us
  Pallas kernels  49.6 us (98%)
  between operations  0.64 us (1%)
    pallas_call x1, Pallas kernels, local(): pl.pallas_call(functools.partial(kernel, dims), out_shape=(jax.ShapeDtype...  46.7 us
    pallas_call x1, Pallas kernels, local(): pl.pallas_call(finish, out_shape=(jax.ShapeDtypeStruct(tok.shape, BF16),...  2.91 us

profile of v1, /device:TPU:0, one launch (start us, length us, event | category | flops | bytes accessed | tf_op | source)
XLA Modules:
  0.0 50.2 jit_solution(7924185072605664994)
XLA Ops:
  0.6 46.7 %shard_map.131 = (bf16[64,4096]{1,0:T(8,128)(2,1)}, bf16[8,4,4,896]{3,2,1,0:T(4,128)(2,1)}, bf16[128,128]{1,0:T(8,128)(2,1)}) custom-call(s32[8,128]{1,0:T(8,128)} %bitcast.2, f32[8,128]{1,0:T(8,128)} %bitcast.3, bf16[64,512]{1,0:T(8,128)(2,1)} %klat_hbm.1, bf16[64,64]{1,0:T(8,128)(2,1)} %krope_hbm.1, bf16[128,7168]{1,0:T(8,128)(2,1)} %tok_hbm.1, ...), custom_call_target="tpu_custom_call" | custom-call | tf_op jit(solution)/shard_map/pallas_call | solution.py:558
  47.3 2.9 %shard_map.132 = (bf16[128,7168]{1,0:T(8,128)(2,1)}, bf16[64,4096]{1,0:T(8,128)(2,1)}) custom-call(bf16[8,4,4,896]{3,2,1,0:T(4,128)(2,1)} %get-tuple-element.7.res_hbm, bf16[128,128]{1,0:T(8,128)(2,1)} %get-tuple-element.8.wmix_hbm, bf16[64,4096]{1,0:T(8,128)(2,1)} %get-tuple-element.9.att_hbm), custom_call_target="tpu_custom_call" | custom-call | tf_op jit(solution)/shard_map/pallas_call | solution.py:614

commit v2 on v1

--- a/solution.py
+++ b/solution.py
@@ -65,18 +65,12 @@
     rbuf,
     load_sem,
     store_sem,
-    kz_send,
-    kx_send,
-    ky_send,
-    kc_send,
+    send_sem,
+    ksend,
     krecv,
-    zsend,
     zrecv,
-    asend,
     arecv,
-    rsend,
     rrecv,
-    bsend,
     brecv,
 ):
     groups, n_sec, rows, heads, lat, ropew, nope, hb = dims
@@ -103,8 +97,6 @@
         index = group * SPLIT + member
         return (index // n_sec, lax.rem(index, n_sec))
 
-    pending = []
-    stores = []
 
     def rcopy(src, dst, ss, rs, target):
         return pltpu.make_async_remote_copy(
@@ -112,16 +104,14 @@
             device_id=target, device_id_type=MESH_ID,
         )
 
-    def send(src, dst, ss, rs, target):
-        cp = rcopy(src, dst, ss, rs, target)
-        cp.start()
-        pending.append(cp)
-        return cp
-
-    def store(src, dst):
-        cp = pltpu.make_async_copy(src, dst, store_sem.at[len(stores)])
-        cp.start()
-        stores.append(cp)
+    def send(src, dst, kind, rs, target):
+        rcopy(src, dst, send_sem.at[kind], rs, target).start()
+
+    def received(like, rs):
+        rcopy(like, like, send_sem.at[0], rs, nx).wait_recv()
+
+    def store(src, dst, kind):
+        pltpu.make_async_copy(src, dst, store_sem.at[kind]).start()
 
     nx, nc, ny = dev(g, mx), dev(g, mc), dev(g, my)
     others = [lax.rem(g + step, groups) for step in range(1, groups)]
@@ -153,34 +143,65 @@
     l_klat.start()
     l_krope.start()
 
-    part_rows = rows // 2
-
-    def kpiece(shard, which):
-        return keys.at[shard, pl.ds(pl.multiple_of(which * part_rows, part_rows), part_rows), pl.ds(0, sent)]
-
     def kwhole(shard):
         return keys.at[shard, :, pl.ds(0, sent)]
 
     def kshard(group, member):
         return (group * SPLIT + member) // n_sec
 
-    def ksend(group, member, which, sem, target):
-        shard = kshard(group, member)
-        piece = kpiece(shard, which)
-        send(piece, piece, sem, krecv.at[shard, which], target)
-
-    def karrive(group, member, which):
-        shard = kshard(group, member)
-        piece = kpiece(shard, which)
-        rcopy(piece, piece, kz_send.at[0], krecv.at[shard, which], nx).wait_recv()
-
-    def ksend_whole(group, member, sem, target):
-        shard = kshard(group, member)
-        send(kwhole(shard), kwhole(shard), sem, krecv.at[shard, 0], target)
-
-    def karrive_whole(group, member):
-        shard = kshard(group, member)
-        rcopy(kwhole(shard), kwhole(shard), kz_send.at[0], krecv.at[shard, 0], nx).wait_recv()
+    def whole(group, member, way, s, target, rs=None):
+        piece = kwhole(kshard(group, member))
+        rcopy(piece, piece, ksend.at[way, s], krecv.at[way, s if rs is None else rs], target).start()
+
+    up = dev(lax.rem(g + 1, groups), m)
+    top_plane = groups - 1
+
+    def guarded(s, fn):
+        if s == 0:
+            fn()
+        else:
+            pl.when(g >= s)(fn)
+
+    def key_up(s, member, way):
+        if s >= top_plane:
+            return
+        cond = g < top_plane if s == 0 else (g >= s) & (g < top_plane)
+
+        @pl.when(cond)
+        def _():
+            whole(g - s, member, way, s, up, s + 1)
+
+    def key_own():
+        whole(g, m, 1, 0, ny)
+        whole(g, m, 3, 0, nc)
+
+    def key_pass(s, member, way):
+        with scope("kp%d_%d" % (s, way)):
+            if s == 0 and way == 0:
+                key_up(0, m, 0)
+                return
+
+            @functools.partial(guarded, s)
+            def _():
+                received(kwhole(0), krecv.at[1 if s == 0 else way, s])
+
+            key_up(s, member, way)
+
+            @functools.partial(guarded, s)
+            def _():
+                whole(g - s, member, 3, s, nc)
+
+    def key_a(s):
+        key_pass(s, m, 0)
+
+    def key_b(s):
+        key_pass(s, my, 2)
+
+    def key_w(s):
+        with scope("kw%d" % s):
+            @functools.partial(guarded, s)
+            def _():
+                received(keys.at[pl.ds(0, 2), :, pl.ds(0, sent)], krecv.at[3, s])
 
     with scope("a_sel"):
         lanes = wmix.shape[1]
@@ -223,10 +244,8 @@
     with scope("d_zsend"):
         for c in range(CHUNKS):
             for i, o in enumerate(others):
-                send(outg.at[c, o], zbuf.at[c, g], zsend.at[c, i], zrecv.at[c, g], dev(o, m))
-        ksend(g, m, bx, ky_send.at[0], ny)
-        for i, o in enumerate(others):
-            ksend_whole(g, m, kz_send.at[i], dev(o, m))
+                send(outg.at[c, o], zbuf.at[c, g], 0, zrecv.at[c], dev(o, m))
+        key_own()
 
     with scope("e_wmix"):
         weight = chosen * gate
@@ -236,7 +255,7 @@
         wmix[...] = jnp.where(
             row < slots, w1, jnp.where(row < 2 * slots, w2, jnp.where(row < 3 * slots, w3, 0.0))
         ).T.astype(BF16)
-        store(wmix, wmix_hbm)
+        store(wmix, wmix_hbm, 0)
 
         maskw = keys.shape[2] - sent
 
@@ -253,6 +272,13 @@
             1.0,
             0.0,
         ).astype(BF16)
+
+    per = SPLIT // n_sec
+    with scope("zero"):
+        for s in range(1, groups):
+            @pl.when(g + s < groups)
+            def _():
+                keys[pl.ds((g + s) * per, per), :, :sent] = jnp.zeros((per, rows, sent), BF16)
 
     with scope("f_loads"):
         l_qn.wait()
@@ -277,47 +303,44 @@
                     qcat[place, lat:sent] = jnp.where(keep, rope.astype(F32), 0.0).astype(BF16)
                     qcat[place, sent:] = unit
 
-    def spread(kind, member, c, target):
+    def spread(member, c, way, target):
         piece = arr.at[c, member]
-        send(piece, piece, asend.at[kind, c], arecv.at[c, member], target)
-
-    def arrive(member, c):
-        piece = arr.at[c, member]
-        rcopy(piece, piece, asend.at[0, c], arecv.at[c, member], nx).wait_recv()
+        send(piece, piece, 1, arecv.at[c, way], target)
+
+    def arrive(c, way):
+        received(arr.at[c, 0] if way < 3 else arr.at[c, pl.ds(0, 4)], arecv.at[c, way])
 
     def start_chunk(c):
         with scope("s%d" % c):
-            for i, o in enumerate(others):
-                rcopy(outg.at[c, o], zbuf.at[c, o], zsend.at[c, i], zrecv.at[c, o], dev(o, m)).wait_recv()
+            received(zbuf.at[c, pl.ds(0, groups - 1)], zrecv.at[c])
             zbuf[c, g] = outg[c, g]
             blocks = [zbuf[c, e].astype(F32) for e in range(groups)]
             arr[c, m] = jnp.concatenate(blocks, axis=0).astype(BF16)
-            spread(0, m, c, nx)
-            spread(1, m, c, ny)
-            spread(2, m, c, nc)
+            spread(m, c, 0, nx)
+            spread(m, c, 1, ny)
+            spread(m, c, 3, nc)
 
     def forward_chunk(c):
         with scope("fw%d" % c):
-            arrive(mx, c)
+            arrive(c, 0)
             if c % 2 == 0:
-                spread(3, mx, c, ny)
-            spread(4, mx, c, nc)
-            arrive(my, c)
+                spread(mx, c, 2, ny)
+            spread(mx, c, 3, nc)
+            arrive(c, 1)
             if c % 2 == 1:
-                spread(3, my, c, nx)
-            spread(5, my, c, nc)
+                spread(my, c, 2, nx)
+            spread(my, c, 3, nc)
 
     count = SPLIT * slots
 
     def finish_chunk(c):
         with scope("fin%d" % c):
-            arrive(mxy, c)
-            spread(6, mxy, c, nc)
+            arrive(c, 2)
+            spread(mxy, c, 3, nc)
 
     def gate_up(c):
         with scope("guw%d" % c):
-            for member in (mc, mx + mc - m, my + mc - m, mxy + mc - m):
-                arrive(member, c)
+            arrive(c, 3)
         with scope("gu%d" % c):
             x = arr[c].reshape(count, cw)
             g_part = jnp.dot(x, gw[c * cw : (c + 1) * cw], preferred_element_type=F32)
@@ -329,110 +352,10 @@
                 acc[0] += g_part
                 acc[1] += u_part
 
-    def kx_own():
-        with scope("kxo"):
-            karrive(g, my, bx)
-            ksend(g, my, bx, kx_send.at[0], nx)
-
-    def ky_step():
-        with scope("ky"):
-            for i, o in enumerate(others):
-                karrive_whole(o, m)
-                ksend(o, m, bx, ky_send.at[i + 1], ny)
-
-    def kx_step():
-        with scope("kx"):
-            for i, o in enumerate(others):
-                karrive(o, my, bx)
-                ksend(o, my, bx, kx_send.at[i + 1], nx)
-
-    def kc_step():
-        with scope("kc"):
-            for i, o in enumerate(every):
-                ksend_whole(o, m, kc_send.at[i, 0], nc)
-            for i, o in enumerate(every):
-                karrive(o, my, 1 - bx)
-                ksend_whole(o, my, kc_send.at[i, 1], nc)
-
-    def key_wait():
-        with scope("kw"):
-            for o in every:
-                for member in (mc, my + mc - m):
-                    karrive_whole(o, member)
-
     pairs_n = heads // 2
 
     def ql(a, b):
         query_latents(a * pairs_n // 8, b * pairs_n // 8)
-
-    ql(0, 3)
-    start_chunk(0)
-    kx_own()
-    ql(3, 4)
-    start_chunk(1)
-    ql(4, 5)
-    forward_chunk(0)
-    start_chunk(2)
-    ql(5, 6)
-    forward_chunk(1)
-    start_chunk(3)
-    finish_chunk(0)
-    ql(6, 7)
-    forward_chunk(2)
-    l_gw.wait()
-    l_uw.wait()
-    finish_chunk(1)
-    gate_up(0)
-    forward_chunk(3)
-    ky_step()
-    finish_chunk(2)
-    gate_up(1)
-    ql(7, 8)
-    finish_chunk(3)
-    gate_up(2)
-    kx_step()
-    gate_up(3)
-    with scope("act"):
-        gate_act = acc[0]
-        hidden = (gate_act / (1.0 + jnp.exp(-gate_act)) * acc[1]).astype(BF16)
-        l_dw.wait()
-
-    c1, c2, c3 = [], [], []
-
-    def down(c):
-        value = jnp.dot(hidden, dw[:, c * rw : (c + 1) * rw], preferred_element_type=F32)
-        part[c] = value.astype(BF16).reshape(2, 2, 2, slots, rw)
-        c1.append(send(part.at[c, :, 1 - bc], r1.at[c], rsend.at[0, c], rrecv.at[0, c], nc))
-
-    def sum_cores(c):
-        with scope("sc%d" % c):
-            c1[c].wait_recv()
-            for a in range(2):
-                for b in range(2):
-                    s1[c, a, b] = (part[c, a, bc, b].astype(F32) + r1[c, a, b].astype(F32)).astype(BF16)
-            src = s1.at[c, :, 1 - bx] if c % 2 == 0 else s1.at[c, 1 - by]
-            c2.append(send(src, r2.at[c], rsend.at[1, c], rrecv.at[1, c], nx if c % 2 == 0 else ny))
-
-    def sum_first(c):
-        with scope("sf%d" % c):
-            c2[c].wait_recv()
-            for a in range(2):
-                mine = s1[c, a, bx] if c % 2 == 0 else s1[c, by, a]
-                s2[c, a] = (mine.astype(F32) + r2[c, a].astype(F32)).astype(BF16)
-            keep = by if c % 2 == 0 else bx
-            c3.append(send(s2.at[c, 1 - keep], r3.at[c], rsend.at[2, c], rrecv.at[2, c],
-                           ny if c % 2 == 0 else nx))
-
-    def sum_second(c):
-        with scope("ss%d" % c):
-            c3[c].wait_recv()
-            keep = by if c % 2 == 0 else bx
-            total = s2[c, keep].astype(F32) + r3[c].astype(F32)
-            for e in range(groups):
-                rbuf[c, e] = total[e * CAP : (e + 1) * CAP].astype(BF16)
-            for i, o in enumerate(others):
-                send(rbuf.at[c, o], res_hbm.at[c, g], bsend.at[c, i], brecv.at[c, g], dev(o, m))
-            store(rbuf.at[c, g], res_hbm.at[c, g])
 
     seq = keys.shape[0] * keys.shape[1]
     block = hb * rows
@@ -461,46 +384,145 @@
                     att_ref[:, pl.ds(pl.multiple_of(h * vdim, vdim), vdim)] = value.astype(BF16)
 
             cols = pl.ds(first * hb * vdim, (last - first) * hb * vdim)
-            store(att_ref.at[:, cols], att_hbm.at[:, cols])
-
-    def pair(fn, k):
-        fn(2 * k)
-        fn(2 * k + 1)
+            store(att_ref.at[:, cols], att_hbm.at[:, cols], 2)
+
+    def far(fn, first):
+        for s in range(first, groups):
+            fn(s)
+
+    ql(0, 4)
+    start_chunk(0)
+    key_a(0)
+    start_chunk(1)
+    key_b(0)
+    ql(4, 5)
+    start_chunk(2)
+    ql(5, 6)
+    start_chunk(3)
+    forward_chunk(0)
+    ql(6, 7)
+    key_a(1)
+    forward_chunk(1)
+    ql(7, 8)
+    forward_chunk(2)
+    key_b(1)
+    forward_chunk(3)
+    finish_chunk(0)
+    key_a(2)
+    finish_chunk(1)
+    key_b(2)
+    finish_chunk(2)
+    l_gw.wait()
+    l_uw.wait()
+    gate_up(0)
+    finish_chunk(3)
+    gate_up(1)
+    gate_up(2)
+    far(key_a, 3)
+    gate_up(3)
+    with scope("act"):
+        gate_act = acc[0]
+        hidden = (gate_act / (1.0 + jnp.exp(-gate_act)) * acc[1]).astype(BF16)
+        l_dw.wait()
+
+    def down(k):
+        value = jnp.dot(hidden, dw[:, k * 2 * rw : (k + 1) * 2 * rw], preferred_element_type=F32)
+        value = value.astype(BF16)
+        for c in (2 * k, 2 * k + 1):
+            start = (c % 2) * rw
+            part[c] = value[:, start : start + rw].reshape(2, 2, 2, slots, rw)
+            send(part.at[c, :, 1 - bc], r1.at[c], 2, rrecv.at[0, k], nc)
+
+    def sum_cores(k):
+        with scope("sc%d" % k):
+            received(r1.at[pl.ds(0, 2)], rrecv.at[0, k])
+            for c in (2 * k, 2 * k + 1):
+                for a in range(2):
+                    for b in range(2):
+                        s1[c, a, b] = (part[c, a, bc, b].astype(F32) + r1[c, a, b].astype(F32)).astype(BF16)
+            send(s1.at[2 * k, :, 1 - bx], r2.at[2 * k], 3, rrecv.at[1, k], nx)
+            send(s1.at[2 * k + 1, 1 - by], r2.at[2 * k + 1], 3, rrecv.at[1, k], ny)
+
+    def sum_first(k):
+        with scope("sf%d" % k):
+            received(r2.at[pl.ds(0, 2)], rrecv.at[1, k])
+            for c in (2 * k, 2 * k + 1):
+                for a in range(2):
+                    mine = s1[c, a, bx] if c % 2 == 0 else s1[c, by, a]
+                    s2[c, a] = (mine.astype(F32) + r2[c, a].astype(F32)).astype(BF16)
+            send(s2.at[2 * k, 1 - by], r3.at[2 * k], 4, rrecv.at[2, k], ny)
+            send(s2.at[2 * k + 1, 1 - bx], r3.at[2 * k + 1], 4, rrecv.at[2, k], nx)
+
+    def sum_second(k):
+        with scope("ss%d" % k):
+            received(r3.at[pl.ds(0, 2)], rrecv.at[2, k])
+            for c in (2 * k, 2 * k + 1):
+                keep = by if c % 2 == 0 else bx
+                total = s2[c, keep].astype(F32) + r3[c].astype(F32)
+                for e in range(groups):
+                    rbuf[c, e] = total[e * CAP : (e + 1) * CAP].astype(BF16)
+                for o in others:
+                    send(rbuf.at[c, o], res_hbm.at[c, g], 5, brecv.at[0], dev(o, m))
+                store(rbuf.at[c, g], res_hbm.at[c, g], 1)
 
     with scope("down"):
-        for c in range(RCHUNKS):
-            down(c)
-    pair(sum_cores, 0)
-    pair(sum_cores, 1)
-    kc_step()
-    pair(sum_first, 0)
-    pair(sum_cores, 2)
+        for k in range(RCHUNKS // 2):
+            down(k)
+    sum_cores(0)
+    sum_cores(1)
+    far(key_b, 3)
     with scope("vuw"):
         l_vu.wait()
-    key_wait()
+    far(key_w, 0)
     attend(0, 1)
-    pair(sum_first, 1)
-    pair(sum_cores, 3)
-    pair(sum_second, 0)
+    sum_first(0)
+    sum_cores(2)
     attend(1, 2)
-    pair(sum_first, 2)
-    pair(sum_second, 1)
+    sum_first(1)
+    sum_cores(3)
+    sum_second(0)
     attend(2, 3)
-    pair(sum_first, 3)
-    pair(sum_second, 2)
-    attend(3, 5)
-    pair(sum_second, 3)
+    sum_first(2)
+    sum_second(1)
+    attend(3, 4)
+    sum_first(3)
+    sum_second(2)
+    attend(4, 5)
+    sum_second(3)
     attend(5, 8)
 
     with scope("z_res"):
-        for c in range(RCHUNKS):
-            for i, o in enumerate(others):
-                rcopy(rbuf.at[c, o], res_hbm.at[c, o], bsend.at[c, i], brecv.at[c, o], dev(o, m)).wait_recv()
+        received(res_hbm.at[:, pl.ds(0, groups - 1)], brecv.at[0])
     with scope("z_sends"):
-        for cp in pending:
-            cp.wait_send()
-        for cp in stores:
-            cp.wait()
+        sources = [
+            outg.at[:, pl.ds(0, groups - 1)],
+            arr.at[:, pl.ds(0, 7)],
+            r1,
+            r2,
+            r3,
+            rbuf.at[:, pl.ds(0, groups - 1)],
+        ]
+        for kind, source in enumerate(sources):
+            rcopy(source, source, send_sem.at[kind], brecv.at[0], nx).wait_send()
+        for s in range(groups):
+            def sent_keys(like, way):
+                rcopy(like, like, ksend.at[way, s], krecv.at[way, s], nx).wait_send()
+
+            if s == 0:
+                sent_keys(kwhole(0), 1)
+            if s < top_plane:
+                @pl.when((g >= s) & (g < top_plane))
+                def _():
+                    sent_keys(kwhole(0), 0)
+                    sent_keys(kwhole(0), 2)
+
+            @functools.partial(guarded, s)
+            def _():
+                sent_keys(keys.at[pl.ds(0, 2), :, pl.ds(0, sent)], 3)
+
+        pltpu.make_async_copy(wmix, wmix_hbm, store_sem.at[0]).wait()
+        pltpu.make_async_copy(rbuf.at[:, 0], res_hbm.at[:, 0], store_sem.at[1]).wait()
+        pltpu.make_async_copy(att_ref, att_hbm, store_sem.at[2]).wait()
 
 
 def finish(res_hbm, wmix_hbm, att_hbm, rout_hbm, out_hbm, res, wmix, att, rout, sem):
@@ -592,20 +614,14 @@
             pltpu.VMEM((RCHUNKS, slots, rw), BF16),
             pltpu.VMEM((RCHUNKS, groups, CAP, rw), BF16),
             dma((11 + CHUNKS,)),
-            dma((1 + RCHUNKS + 8,)),
-            dma((groups,)),
-            dma((groups,)),
-            dma((groups,)),
-            dma((groups, 2)),
-            dma((n_ctx, 2)),
-            dma((CHUNKS, groups)),
-            dma((CHUNKS, groups)),
-            dma((7, CHUNKS)),
-            dma((CHUNKS, SPLIT)),
-            dma((3, RCHUNKS)),
-            dma((3, RCHUNKS)),
-            dma((RCHUNKS, groups)),
-            dma((RCHUNKS, groups)),
+            dma((3,)),
+            dma((6,)),
+            dma((4, groups)),
+            dma((4, groups)),
+            dma((CHUNKS,)),
+            dma((CHUNKS, 4)),
+            dma((3, RCHUNKS // 2)),
+            dma((1,)),
         ],
         compiler_params=pltpu.CompilerParams(
             collective_id=0, has_side_effects=True, vmem_limit_bytes=67043328

time: 50.4 us -> 44.5 us (0.88)
  Pallas kernels: 49.6 us -> 43.7 us
    pallas_call x1, Pallas kernels: 46.7 us -> 40.8 us  [local(): pl.pallas_call(functools.partial(kernel, dims), out_shape=(jax.ShapeDtype...]
where the time goes in v2:
time: 44.5 us; the launch traced here: 44.4 us
  Pallas kernels  43.7 us (98%)
  between operations  0.64 us (1%)
    pallas_call x1, Pallas kernels, local(): pl.pallas_call(functools.partial(kernel, dims), out_shape=(jax.ShapeDtype...  40.8 us
    pallas_call x1, Pallas kernels, local(): pl.pallas_call(finish, out_shape=(jax.ShapeDtypeStruct(tok.shape, BF16),...  2.9 us

profile of v2, /device:TPU:0, one launch (start us, length us, event | category | flops | bytes accessed | tf_op | source)
XLA Modules:
  0.0 44.4 jit_solution(4025425355955065419)
XLA Ops:
  0.6 40.8 %shard_map.131 = (bf16[64,4096]{1,0:T(8,128)(2,1)}, bf16[8,4,4,896]{3,2,1,0:T(4,128)(2,1)}, bf16[128,128]{1,0:T(8,128)(2,1)}) custom-call(s32[8,128]{1,0:T(8,128)} %bitcast.2, f32[8,128]{1,0:T(8,128)} %bitcast.3, bf16[64,512]{1,0:T(8,128)(2,1)} %klat_hbm.1, bf16[64,64]{1,0:T(8,128)(2,1)} %krope_hbm.1, bf16[128,7168]{1,0:T(8,128)(2,1)} %tok_hbm.1, ...), custom_call_target="tpu_custom_call" | custom-call | tf_op jit(solution)/shard_map/pallas_call | solution.py:580
  41.4 2.9 %shard_map.132 = (bf16[128,7168]{1,0:T(8,128)(2,1)}, bf16[64,4096]{1,0:T(8,128)(2,1)}) custom-call(bf16[8,4,4,896]{3,2,1,0:T(4,128)(2,1)} %get-tuple-element.7.res_hbm, bf16[128,128]{1,0:T(8,128)(2,1)} %get-tuple-element.8.wmix_hbm, bf16[64,4096]{1,0:T(8,128)(2,1)} %get-tuple-element.9.att_hbm), custom_call_target="tpu_custom_call" | custom-call | tf_op jit(solution)/shard_map/pallas_call | solution.py:630

commit v3 on v2

--- a/solution.py
+++ b/solution.py
@@ -11,7 +11,7 @@
 SPLIT = 8
 CHUNKS = 4
 RCHUNKS = 8
-PIECES = 4
+PIECES = 2
 LOG2E = 1.4426950408889634
 MESH_ID = pl.DeviceIdType.MESH
 F32 = jnp.float32
@@ -149,9 +149,12 @@
     def kshard(group, member):
         return (group * SPLIT + member) // n_sec
 
+    def kslot(way, s):
+        return (groups + 1, groups, 2 * groups + 1, 0)[way] + s
+
     def whole(group, member, way, s, target, rs=None):
         piece = kwhole(kshard(group, member))
-        rcopy(piece, piece, ksend.at[way, s], krecv.at[way, s if rs is None else rs], target).start()
+        rcopy(piece, piece, ksend.at[kslot(way, s)], krecv.at[kslot(way, s if rs is None else rs)], target).start()
 
     up = dev(lax.rem(g + 1, groups), m)
     top_plane = groups - 1
@@ -183,7 +186,7 @@
 
             @functools.partial(guarded, s)
             def _():
-                received(kwhole(0), krecv.at[1 if s == 0 else way, s])
+                received(kwhole(0), krecv.at[kslot(1 if s == 0 else way, s)])
 
             key_up(s, member, way)
 
@@ -201,7 +204,7 @@
         with scope("kw%d" % s):
             @functools.partial(guarded, s)
             def _():
-                received(keys.at[pl.ds(0, 2), :, pl.ds(0, sent)], krecv.at[3, s])
+                received(keys.at[pl.ds(0, 2), :, pl.ds(0, sent)], krecv.at[kslot(3, s)])
 
     with scope("a_sel"):
         lanes = wmix.shape[1]
@@ -358,15 +361,14 @@
         query_latents(a * pairs_n // 8, b * pairs_n // 8)
 
     seq = keys.shape[0] * keys.shape[1]
-    block = hb * rows
     scale = (nope + ropew) ** -0.5 * LOG2E
-    nb = heads // hb
     vdim = vu.shape[2]
 
-    def attend(a, b):
-        first, last = a * nb // 8, b * nb // 8
-        with scope("att%d" % a):
-            @pl.loop(first, last)
+    def attend(first, last, most):
+        size = min(hb, most)
+        block = size * rows
+        with scope("att%d" % first):
+            @pl.loop(first // size, last // size)
             def _(b):
                 q = qcat[pl.ds(pl.multiple_of(b * block, block), block)]
                 kk = keys[...].reshape(seq, keys.shape[2])
@@ -376,14 +378,14 @@
                 total = jnp.sum(expo, axis=1, keepdims=True)
                 mixed = jnp.dot(expo.astype(BF16), kk[:, :lat], preferred_element_type=F32)
                 mixed = (mixed / total).astype(BF16)
-                for k in range(hb):
-                    h = b * hb + k
+                for k in range(size):
+                    h = b * size + k
                     value = jnp.dot(
                         mixed[k * rows : (k + 1) * rows], vu[h], preferred_element_type=F32
                     )
                     att_ref[:, pl.ds(pl.multiple_of(h * vdim, vdim), vdim)] = value.astype(BF16)
 
-            cols = pl.ds(first * hb * vdim, (last - first) * hb * vdim)
+            cols = pl.ds(first * vdim, (last - first) * vdim)
             store(att_ref.at[:, cols], att_hbm.at[:, cols], 2)
 
     def far(fn, first):
@@ -408,17 +410,16 @@
     key_b(1)
     forward_chunk(3)
     finish_chunk(0)
+    finish_chunk(1)
     key_a(2)
-    finish_chunk(1)
-    key_b(2)
     finish_chunk(2)
     l_gw.wait()
     l_uw.wait()
     gate_up(0)
+    key_b(2)
     finish_chunk(3)
     gate_up(1)
     gate_up(2)
-    far(key_a, 3)
     gate_up(3)
     with scope("act"):
         gate_act = acc[0]
@@ -468,28 +469,28 @@
     with scope("down"):
         for k in range(RCHUNKS // 2):
             down(k)
+    far(key_a, 3)
     sum_cores(0)
     sum_cores(1)
     far(key_b, 3)
     with scope("vuw"):
         l_vu.wait()
     far(key_w, 0)
-    attend(0, 1)
+    attend(heads * 0 // 32, heads * 4 // 32, 4)
     sum_first(0)
     sum_cores(2)
-    attend(1, 2)
     sum_first(1)
     sum_cores(3)
+    attend(heads * 4 // 32, heads * 8 // 32, 4)
     sum_second(0)
-    attend(2, 3)
     sum_first(2)
+    attend(heads * 8 // 32, heads * 12 // 32, 4)
     sum_second(1)
-    attend(3, 4)
     sum_first(3)
+    attend(heads * 12 // 32, heads * 16 // 32, 4)
     sum_second(2)
-    attend(4, 5)
     sum_second(3)
-    attend(5, 8)
+    attend(heads * 16 // 32, heads * 32 // 32, 16)
 
     with scope("z_res"):
         received(res_hbm.at[:, pl.ds(0, groups - 1)], brecv.at[0])
@@ -506,7 +507,7 @@
             rcopy(source, source, send_sem.at[kind], brecv.at[0], nx).wait_send()
         for s in range(groups):
             def sent_keys(like, way):
-                rcopy(like, like, ksend.at[way, s], krecv.at[way, s], nx).wait_send()
+                rcopy(like, like, ksend.at[kslot(way, s)], krecv.at[0], nx).wait_send()
 
             if s == 0:
                 sent_keys(kwhole(0), 1)
@@ -537,10 +538,12 @@
         loads[p].start()
     a_load = pltpu.make_async_copy(att_hbm, att, sem.at[1 + PIECES])
     a_load.start()
-    w_load.wait()
+    with scope("fw"):
+        w_load.wait()
     stores = []
     for p in range(PIECES):
-        loads[p].wait()
+        with scope("fl%d" % p):
+            loads[p].wait()
         for c in range(p * step, (p + 1) * step):
             blocks = [res[c, e].astype(F32) for e in range(groups)]
             block_rows = jnp.concatenate(blocks, axis=0).astype(BF16)
@@ -553,11 +556,13 @@
             pltpu.make_async_copy(rout.at[:, cols], rout_hbm.at[:, cols], sem.at[2 + PIECES + p])
         )
         stores[p].start()
-    a_load.wait()
-    stores.append(pltpu.make_async_copy(att, out_hbm, sem.at[2 + 2 * PIECES]))
-    stores[-1].start()
-    for cp in stores:
-        cp.wait()
+        if p == 0:
+            a_load.wait()
+            a_store = pltpu.make_async_copy(att, out_hbm, sem.at[2 + 2 * PIECES])
+            a_store.start()
+    with scope("fz"):
+        for cp in stores + [a_store]:
+            cp.wait()
 
 
 def local(n_ctx, n_sec, qn, qr, klat, krope, ku, vu, tok, ids, gates, gw, uw, dw):
@@ -571,7 +576,7 @@
     cw = width // CHUNKS
     rw = width // RCHUNKS
     kw = lat + 2 * ropew + 128
-    hb = 4 if n_ctx * rows <= 2048 else 1
+    hb = 16 if n_ctx * rows <= 2048 else 1
     lanes = -(-3 * slots // 128) * 128
     dims = (groups, n_sec, rows, heads, lat, ropew, nope, hb)
     a = pl.BlockSpec(memory_space=pl.ANY)
@@ -616,8 +621,8 @@
             dma((11 + CHUNKS,)),
             dma((3,)),
             dma((6,)),
-            dma((4, groups)),
-            dma((4, groups)),
+            dma((3 * groups + 1,)),
+            dma((3 * groups + 1,)),
             dma((CHUNKS,)),
             dma((CHUNKS, 4)),
             dma((3, RCHUNKS // 2)),

time: 44.5 us -> 43.7 us (0.982)
  Pallas kernels: 43.7 us -> 42.9 us
    pallas_call x1, Pallas kernels: 40.8 us -> 40.1 us  [local(): pl.pallas_call(functools.partial(kernel, dims), out_shape=(jax.ShapeDtype...]
where the time goes in v3:
time: 43.7 us; the launch traced here: 43.5 us
  Pallas kernels  42.9 us (98%)
  between operations  0.64 us (1%)
    pallas_call x1, Pallas kernels, local(): pl.pallas_call(functools.partial(kernel, dims), out_shape=(jax.ShapeDtype...  40.1 us
    pallas_call x1, Pallas kernels, local(): pl.pallas_call(finish, out_shape=(jax.ShapeDtypeStruct(tok.shape, BF16),...  2.76 us

profile of v3, /device:TPU:0, one launch (start us, length us, event | category | flops | bytes accessed | tf_op | source)
XLA Modules:
  0.0 43.5 jit_solution(17660297463931996952)
XLA Ops:
  0.6 40.1 %shard_map.131 = (bf16[64,4096]{1,0:T(8,128)(2,1)}, bf16[8,4,4,896]{3,2,1,0:T(4,128)(2,1)}, bf16[128,128]{1,0:T(8,128)(2,1)}) custom-call(s32[8,128]{1,0:T(8,128)} %bitcast.2, f32[8,128]{1,0:T(8,128)} %bitcast.3, bf16[64,512]{1,0:T(8,128)(2,1)} %klat_hbm.1, bf16[64,64]{1,0:T(8,128)(2,1)} %krope_hbm.1, bf16[128,7168]{1,0:T(8,128)(2,1)} %tok_hbm.1, ...), custom_call_target="tpu_custom_call" | custom-call | tf_op jit(solution)/shard_map/pallas_call | solution.py:585
  40.8 2.8 %shard_map.132 = (bf16[128,7168]{1,0:T(8,128)(2,1)}, bf16[64,4096]{1,0:T(8,128)(2,1)}) custom-call(bf16[8,4,4,896]{3,2,1,0:T(4,128)(2,1)} %get-tuple-element.7.res_hbm, bf16[128,128]{1,0:T(8,128)(2,1)} %get-tuple-element.8.wmix_hbm, bf16[64,4096]{1,0:T(8,128)(2,1)} %get-tuple-element.9.att_hbm), custom_call_target="tpu_custom_call" | custom-call | tf_op jit(solution)/shard_map/pallas_call | solution.py:635

commit v4 on v3

--- a/solution.py
+++ b/solution.py
@@ -53,7 +53,7 @@
     qcat,
     keys,
     outg,
-    zbuf,
+    own,
     arr,
     acc,
     part,
@@ -69,6 +69,7 @@
     ksend,
     krecv,
     zrecv,
+    orecv,
     arecv,
     rrecv,
     brecv,
@@ -247,7 +248,11 @@
     with scope("d_zsend"):
         for c in range(CHUNKS):
             for i, o in enumerate(others):
-                send(outg.at[c, o], zbuf.at[c, g], 0, zrecv.at[c], dev(o, m))
+                send(outg.at[c, o], arr.at[c, m, groups - 2 - i], 0, zrecv.at[c], dev(o, m))
+        own[m] = outg[:, g]
+        for way, target in enumerate((nx, ny)):
+            send(own.at[m], own.at[m], 6, orecv.at[way], target)
+        send(own.at[m], own.at[m], 6, orecv.at[3], nc)
         key_own()
 
     with scope("e_wmix"):
@@ -315,10 +320,7 @@
 
     def start_chunk(c):
         with scope("s%d" % c):
-            received(zbuf.at[c, pl.ds(0, groups - 1)], zrecv.at[c])
-            zbuf[c, g] = outg[c, g]
-            blocks = [zbuf[c, e].astype(F32) for e in range(groups)]
-            arr[c, m] = jnp.concatenate(blocks, axis=0).astype(BF16)
+            received(arr.at[c, 0], zrecv.at[c])
             spread(m, c, 0, nx)
             spread(m, c, 1, ny)
             spread(m, c, 3, nc)
@@ -334,7 +336,27 @@
                 spread(my, c, 2, nx)
             spread(my, c, 3, nc)
 
-    count = SPLIT * slots
+    half = CHUNKS // 2
+
+    def own_forward():
+        with scope("ofw"):
+            received(own.at[0], orecv.at[0])
+            low = own.at[mx, pl.ds(0, half)]
+            send(low, low, 6, orecv.at[2], ny)
+            send(own.at[mx], own.at[mx], 6, orecv.at[3], nc)
+            received(own.at[0], orecv.at[1])
+            high = own.at[my, pl.ds(half, CHUNKS - half)]
+            send(high, high, 6, orecv.at[2], nx)
+            send(own.at[my], own.at[my], 6, orecv.at[3], nc)
+
+    def own_finish():
+        with scope("ofin"):
+            received(own.at[0], orecv.at[2])
+            send(own.at[mxy], own.at[mxy], 6, orecv.at[3], nc)
+
+    def own_wait():
+        with scope("ow"):
+            received(own.at[pl.ds(0, 4)], orecv.at[3])
 
     def finish_chunk(c):
         with scope("fin%d" % c):
@@ -345,7 +367,11 @@
         with scope("guw%d" % c):
             arrive(c, 3)
         with scope("gu%d" % c):
-            x = arr[c].reshape(count, cw)
+            blocks = []
+            for member in range(SPLIT):
+                blocks.append(own[member, c].astype(F32))
+                blocks += [arr[c, member, i].astype(F32) for i in range(groups - 1)]
+            x = jnp.concatenate(blocks, axis=0).astype(BF16)
             g_part = jnp.dot(x, gw[c * cw : (c + 1) * cw], preferred_element_type=F32)
             u_part = jnp.dot(x, uw[c * cw : (c + 1) * cw], preferred_element_type=F32)
             if c == 0:
@@ -395,12 +421,14 @@
     ql(0, 4)
     start_chunk(0)
     key_a(0)
+    own_forward()
     start_chunk(1)
     key_b(0)
     ql(4, 5)
     start_chunk(2)
     ql(5, 6)
     start_chunk(3)
+    own_finish()
     forward_chunk(0)
     ql(6, 7)
     key_a(1)
@@ -415,6 +443,7 @@
     finish_chunk(2)
     l_gw.wait()
     l_uw.wait()
+    own_wait()
     gate_up(0)
     key_b(2)
     finish_chunk(3)
@@ -462,9 +491,9 @@
                 total = s2[c, keep].astype(F32) + r3[c].astype(F32)
                 for e in range(groups):
                     rbuf[c, e] = total[e * CAP : (e + 1) * CAP].astype(BF16)
-                for o in others:
-                    send(rbuf.at[c, o], res_hbm.at[c, g], 5, brecv.at[0], dev(o, m))
-                store(rbuf.at[c, g], res_hbm.at[c, g], 1)
+                for i, o in enumerate(others):
+                    send(rbuf.at[c, i + 1], res_hbm.at[c, g], 5, brecv.at[0], dev(o, m))
+                store(rbuf.at[c, 0], res_hbm.at[c, g], 1)
 
     with scope("down"):
         for k in range(RCHUNKS // 2):
@@ -472,25 +501,26 @@
     far(key_a, 3)
     sum_cores(0)
     sum_cores(1)
+    sum_cores(2)
     far(key_b, 3)
     with scope("vuw"):
         l_vu.wait()
     far(key_w, 0)
-    attend(heads * 0 // 32, heads * 4 // 32, 4)
+    attend(heads * 0 // 32, heads * 8 // 32, 8)
     sum_first(0)
-    sum_cores(2)
+    sum_cores(3)
+    attend(heads * 8 // 32, heads * 12 // 32, 4)
     sum_first(1)
-    sum_cores(3)
-    attend(heads * 4 // 32, heads * 8 // 32, 4)
+    attend(heads * 12 // 32, heads * 16 // 32, 4)
+    sum_first(2)
     sum_second(0)
-    sum_first(2)
-    attend(heads * 8 // 32, heads * 12 // 32, 4)
+    attend(heads * 16 // 32, heads * 20 // 32, 4)
+    sum_first(3)
     sum_second(1)
-    sum_first(3)
-    attend(heads * 12 // 32, heads * 16 // 32, 4)
     sum_second(2)
+    attend(heads * 20 // 32, heads * 24 // 32, 4)
     sum_second(3)
-    attend(heads * 16 // 32, heads * 32 // 32, 16)
+    attend(heads * 24 // 32, heads * 32 // 32, 8)
 
     with scope("z_res"):
         received(res_hbm.at[:, pl.ds(0, groups - 1)], brecv.at[0])
@@ -502,6 +532,7 @@
             r2,
             r3,
             rbuf.at[:, pl.ds(0, groups - 1)],
+            own.at[pl.ds(0, 7)],
         ]
         for kind, source in enumerate(sources):
             rcopy(source, source, send_sem.at[kind], brecv.at[0], nx).wait_send()
@@ -608,8 +639,8 @@
             pltpu.VMEM((heads * rows, kw), BF16),
             pltpu.VMEM((n_ctx, rows, kw), BF16),
             pltpu.VMEM((CHUNKS, groups, CAP, cw), BF16),
-            pltpu.VMEM((CHUNKS, groups, CAP, cw), BF16),
-            pltpu.VMEM((CHUNKS, SPLIT, slots, cw), BF16),
+            pltpu.VMEM((SPLIT, CHUNKS, CAP, cw), BF16),
+            pltpu.VMEM((CHUNKS, SPLIT, groups - 1, CAP, cw), BF16),
             pltpu.VMEM((2, SPLIT * slots, gw.shape[1]), F32),
             pltpu.VMEM((RCHUNKS, 2, 2, 2, slots, rw), BF16),
             pltpu.VMEM((RCHUNKS, 2, 2, slots, rw), BF16),
@@ -620,10 +651,11 @@
             pltpu.VMEM((RCHUNKS, groups, CAP, rw), BF16),
             dma((11 + CHUNKS,)),
             dma((3,)),
-            dma((6,)),
+            dma((7,)),
             dma((3 * groups + 1,)),
             dma((3 * groups + 1,)),
             dma((CHUNKS,)),
+            dma((4,)),
             dma((CHUNKS, 4)),
             dma((3, RCHUNKS // 2)),
             dma((1,)),

time: 43.7 us -> 42.5 us (0.973)
  Pallas kernels: 42.9 us -> 41.7 us
    pallas_call x1, Pallas kernels: 40.1 us -> 38.9 us  [local(): pl.pallas_call(functools.partial(kernel, dims), out_shape=(jax.ShapeDtype...]
where the time goes in v4:
time: 42.5 us; the launch traced here: 42.3 us
  Pallas kernels  41.7 us (98%)
  between operations  0.64 us (2%)
    pallas_call x1, Pallas kernels, local(): pl.pallas_call(functools.partial(kernel, dims), out_shape=(jax.ShapeDtype...  38.9 us
    pallas_call x1, Pallas kernels, local(): pl.pallas_call(finish, out_shape=(jax.ShapeDtypeStruct(tok.shape, BF16),...  2.76 us

profile of v4, /device:TPU:0, one launch (start us, length us, event | category | flops | bytes accessed | tf_op | source)
XLA Modules:
  0.0 42.3 jit_solution(9268905586224975498)
XLA Ops:
  0.6 38.9 %shard_map.131 = (bf16[64,4096]{1,0:T(8,128)(2,1)}, bf16[8,4,4,896]{3,2,1,0:T(4,128)(2,1)}, bf16[128,128]{1,0:T(8,128)(2,1)}) custom-call(s32[8,128]{1,0:T(8,128)} %bitcast.2, f32[8,128]{1,0:T(8,128)} %bitcast.3, bf16[64,512]{1,0:T(8,128)(2,1)} %klat_hbm.1, bf16[64,64]{1,0:T(8,128)(2,1)} %krope_hbm.1, bf16[128,7168]{1,0:T(8,128)(2,1)} %tok_hbm.1, ...), custom_call_target="tpu_custom_call" | custom-call | tf_op jit(solution)/shard_map/pallas_call | solution.py:616
  39.6 2.8 %shard_map.132 = (bf16[128,7168]{1,0:T(8,128)(2,1)}, bf16[64,4096]{1,0:T(8,128)(2,1)}) custom-call(bf16[8,4,4,896]{3,2,1,0:T(4,128)(2,1)} %get-tuple-element.7.res_hbm, bf16[128,128]{1,0:T(8,128)(2,1)} %get-tuple-element.8.wmix_hbm, bf16[64,4096]{1,0:T(8,128)(2,1)} %get-tuple-element.9.att_hbm), custom_call_target="tpu_custom_call" | custom-call | tf_op jit(solution)/shard_map/pallas_call | solution.py:667

commit v5 on v4

--- a/solution.py
+++ b/solution.py
@@ -491,7 +491,7 @@
                 total = s2[c, keep].astype(F32) + r3[c].astype(F32)
                 for e in range(groups):
                     rbuf[c, e] = total[e * CAP : (e + 1) * CAP].astype(BF16)
-                for i, o in enumerate(others):
+                for i, o in reversed(list(enumerate(others))):
                     send(rbuf.at[c, i + 1], res_hbm.at[c, g], 5, brecv.at[0], dev(o, m))
                 store(rbuf.at[c, 0], res_hbm.at[c, g], 1)
 
@@ -502,25 +502,24 @@
     sum_cores(0)
     sum_cores(1)
     sum_cores(2)
+    sum_cores(3)
     far(key_b, 3)
     with scope("vuw"):
         l_vu.wait()
     far(key_w, 0)
     attend(heads * 0 // 32, heads * 8 // 32, 8)
     sum_first(0)
-    sum_cores(3)
     attend(heads * 8 // 32, heads * 12 // 32, 4)
     sum_first(1)
     attend(heads * 12 // 32, heads * 16 // 32, 4)
     sum_first(2)
     sum_second(0)
-    attend(heads * 16 // 32, heads * 20 // 32, 4)
     sum_first(3)
     sum_second(1)
+    attend(heads * 16 // 32, heads * 20 // 32, 4)
     sum_second(2)
-    attend(heads * 20 // 32, heads * 24 // 32, 4)
     sum_second(3)
-    attend(heads * 24 // 32, heads * 32 // 32, 8)
+    attend(heads * 20 // 32, heads * 32 // 32, 4)
 
     with scope("z_res"):
         received(res_hbm.at[:, pl.ds(0, groups - 1)], brecv.at[0])

time: 42.5 us -> 42.4 us (level)
  no operation moved by 1% of the time
where the time goes in v5:
time: 42.4 us; the launch traced here: 42.2 us
  Pallas kernels  41.6 us (98%)
  between operations  0.64 us (2%)
    pallas_call x1, Pallas kernels, local(): pl.pallas_call(functools.partial(kernel, dims), out_shape=(jax.ShapeDtype...  38.8 us
    pallas_call x1, Pallas kernels, local(): pl.pallas_call(finish, out_shape=(jax.ShapeDtypeStruct(tok.shape, BF16),...  2.76 us

profile of v5, /device:TPU:0, one launch (start us, length us, event | category | flops | bytes accessed | tf_op | source)
XLA Modules:
  0.0 42.2 jit_solution(9359063860218253205)
XLA Ops:
  0.6 38.8 %shard_map.131 = (bf16[64,4096]{1,0:T(8,128)(2,1)}, bf16[8,4,4,896]{3,2,1,0:T(4,128)(2,1)}, bf16[128,128]{1,0:T(8,128)(2,1)}) custom-call(s32[8,128]{1,0:T(8,128)} %bitcast.2, f32[8,128]{1,0:T(8,128)} %bitcast.3, bf16[64,512]{1,0:T(8,128)(2,1)} %klat_hbm.1, bf16[64,64]{1,0:T(8,128)(2,1)} %krope_hbm.1, bf16[128,7168]{1,0:T(8,128)(2,1)} %tok_hbm.1, ...), custom_call_target="tpu_custom_call" | custom-call | tf_op jit(solution)/shard_map/pallas_call | solution.py:615
  39.5 2.8 %shard_map.132 = (bf16[128,7168]{1,0:T(8,128)(2,1)}, bf16[64,4096]{1,0:T(8,128)(2,1)}) custom-call(bf16[8,4,4,896]{3,2,1,0:T(4,128)(2,1)} %get-tuple-element.7.res_hbm, bf16[128,128]{1,0:T(8,128)(2,1)} %get-tuple-element.8.wmix_hbm, bf16[64,4096]{1,0:T(8,128)(2,1)} %get-tuple-element.9.att_hbm), custom_call_target="tpu_custom_call" | custom-call | tf_op jit(solution)/shard_map/pallas_call | solution.py:666
